TPU v7x, 32 devices: a whole 2x2x4 slice. The times are simulated.
32 devices in a mesh: dp: 8 (over y, x, core), mp: 4 (over z).
Axes of the slice: x: 2, y: 2, z: 4, core: 2. Of those that a mesh axis runs over, the one named last changes fastest.
Arguments:
- tokens: bfloat16 [12288, 1792], P(('dp', 'mp')), may hold values from -6 to 6
- cotangent: bfloat16 [12288, 1792], P(('dp', 'mp')), may hold values from -6 to 6
- route: int32 [12288], P(('dp', 'mp')), may hold values from 0 to 12287, as said below
- lengths: int32 [8, 3], P('dp'), may hold values from 1 to 1024, 1536 in all within a row
- key_mask: int32 [12288], P('dp'), may hold values 0 or 1
- norm1_gain: float32 [1792], replicated, may hold values from 0.1 to 1.9
- norm2_gain: float32 [1792], replicated, may hold values from 0.1 to 1.9
- w_query: bfloat16 [1792, 1792], P(None, 'mp'), may hold values from -0.1875 to 0.1875
- w_key: bfloat16 [1792, 1792], P(None, 'mp'), may hold values from -0.1875 to 0.1875
- w_value: bfloat16 [1792, 1792], P(None, 'mp'), may hold values from -0.125 to 0.125
- w_out: bfloat16 [1792, 1792], P('mp'), may hold values from -0.375 to 0.375
- w_gate: bfloat16 [1792, 4096], P(None, 'mp'), may hold values from -0.125 to 0.125
- w_up: bfloat16 [1792, 4096], P(None, 'mp'), may hold values from -0.125 to 0.125
- w_down: bfloat16 [4096, 1792], P('mp'), may hold values from -0.125 to 0.125
Outputs:
- output: bfloat16 [12288, 1792], P(('dp', 'mp'))
- input_grad: bfloat16 [12288, 1792], P(('dp', 'mp'))
- norm1_gain_grad: float32 [1792], replicated
- norm2_gain_grad: float32 [1792], replicated
- w_query_grad: float32 [1792, 1792], P(None, 'mp')
- w_key_grad: float32 [1792, 1792], P(None, 'mp')
- w_value_grad: float32 [1792, 1792], P(None, 'mp')
- w_out_grad: float32 [1792, 1792], P('mp')
- w_gate_grad: float32 [1792, 4096], P(None, 'mp')
- w_up_grad: float32 [1792, 4096], P(None, 'mp')
- w_down_grad: float32 [4096, 1792], P('mp')
Inputs may be any that keep to these rules, and one draw needn't show every extreme that they name: route is a permutation of the 12288 slots. For every row r, slot s = route[r] lies on index s // 1536 of dp and on index (s // 384) % (number of mp indices) of mp, and that mp index equals the mp index of the device that holds row r in given order; every device holds exactly 48 rows bound for each index of dp. Each row of lengths sums to 1536; its largest entry is exactly 1024.
All inputs are finite; a program needn't handle non-finite values. No bound on the sum of `key_mask` on one device may be relied on, other than what follows from the above.
Results may differ from a plain program's by a relative error of at most 0.019.
Values may be sent and summed in bfloat16 or wider, within the bound.
A program may use at most 192 MiB of HBM per device.

v0:
```python
import jax
import jax.numpy as jnp
from jax import lax
from jax.sharding import PartitionSpec as P

HEAD_DIM = 112
WINDOW = 64
TOK_DEV = 1536
EPSILON = 1e-05
MASKED = 1e30


def norm_rows(values):
    inverse = lax.rsqrt(jnp.mean(values * values, axis=-1, keepdims=True) + EPSILON)
    return (values * inverse, inverse)


def norm_back(gradient, normed, inverse, norm_gain):
    scaled = gradient * norm_gain
    result = inverse * (scaled - normed * jnp.mean(scaled * normed, axis=-1, keepdims=True))
    return (result, jnp.sum(gradient * normed, axis=0))


def padded(values, filler):
    front = jnp.full((WINDOW,) + values.shape[1:], filler, values.dtype)
    return jnp.concatenate([front, values], axis=0)


def block_scores(query_block, key_block, query_seg, key_seg, key_flag, first_row, score_scale):
    query_pos = first_row + jnp.arange(query_block.shape[0], dtype=jnp.int32)
    key_pos = first_row - WINDOW + jnp.arange(key_block.shape[0], dtype=jnp.int32)
    distance = query_pos[:, None] - key_pos[None, :]
    allowed = (distance >= 0) & (distance < WINDOW) & (query_seg[:, None] == key_seg[None, :])
    allowed = allowed & ((key_flag[None, :] == 1) | (distance == 0))
    raw_scores = (
        jnp.einsum("qhd,khd->hqk", query_block, key_block, preferred_element_type=jnp.float32)
        * score_scale
    )
    return jnp.where(allowed[None], raw_scores, -MASKED)


def block_inputs(query, key_pad, value_pad, segment, seg_pad, live_pad, first_row, block_rows):
    key_span = block_rows + WINDOW
    return (
        lax.dynamic_slice_in_dim(query, first_row, block_rows, 0),
        lax.dynamic_slice_in_dim(key_pad, first_row, key_span, 0),
        lax.dynamic_slice_in_dim(value_pad, first_row, key_span, 0),
        lax.dynamic_slice_in_dim(segment, first_row, block_rows, 0),
        lax.dynamic_slice_in_dim(seg_pad, first_row, key_span, 0),
        lax.dynamic_slice_in_dim(live_pad, first_row, key_span, 0),
    )


def attend_forward(query, key_all, value_all, segment, key_live):
    token_count, head_count, head_width = query.shape
    block_rows = min(512, token_count)
    score_scale = head_width ** (-0.5)
    key_pad = padded(key_all, 0.0)
    value_pad = padded(value_all, 0.0)
    seg_pad = padded(segment, -1)
    live_pad = padded(key_live, 0)

    def one_block(running, block_index):
        first_row = block_index * block_rows
        query_block, key_block, value_block, query_seg, key_seg, key_flag = block_inputs(
            query, key_pad, value_pad, segment, seg_pad, live_pad, first_row, block_rows
        )
        scores = block_scores(
            query_block, key_block, query_seg, key_seg, key_flag, first_row, score_scale
        )
        row_max = jnp.max(scores, axis=-1, keepdims=True)
        weights = jnp.exp(scores - row_max)
        denominator = jnp.sum(weights, axis=-1, keepdims=True)
        chances = (weights / denominator).astype(jnp.bfloat16)
        mixed = jnp.einsum("hqk,khd->qhd", chances, value_block, preferred_element_type=jnp.float32)
        return (
            running,
            (mixed.astype(jnp.bfloat16), row_max[..., 0] + jnp.log(denominator[..., 0])),
        )

    _, (mixed, logsum) = lax.scan(
        one_block, jnp.zeros((), jnp.int32), jnp.arange(token_count // block_rows, dtype=jnp.int32)
    )
    return (mixed.reshape(token_count, head_count * head_width), logsum)


def attend_backward(query, key_all, value_all, segment, key_live, logsum, mixed_grad):
    token_count, head_count, head_width = query.shape
    block_rows = min(512, token_count)
    key_span = block_rows + WINDOW
    score_scale = head_width ** (-0.5)
    key_pad = padded(key_all, 0.0)
    value_pad = padded(value_all, 0.0)
    seg_pad = padded(segment, -1)
    live_pad = padded(key_live, 0)

    def one_block(running, inputs):
        key_grad, value_grad = running
        block_index, block_logsum = inputs
        first_row = block_index * block_rows
        query_block, key_block, value_block, query_seg, key_seg, key_flag = block_inputs(
            query, key_pad, value_pad, segment, seg_pad, live_pad, first_row, block_rows
        )
        grad_block = lax.dynamic_slice_in_dim(mixed_grad, first_row, block_rows, 0)
        scores = block_scores(
            query_block, key_block, query_seg, key_seg, key_flag, first_row, score_scale
        )
        chances = jnp.exp(scores - block_logsum[..., None])
        chance_grad = jnp.einsum(
            "qhd,khd->hqk", grad_block, value_block, preferred_element_type=jnp.float32
        )
        row_dot = jnp.sum(chances * chance_grad, axis=-1, keepdims=True)
        score_grad = (chances * (chance_grad - row_dot)).astype(jnp.bfloat16)
        query_grad = (
            jnp.einsum("hqk,khd->qhd", score_grad, key_block, preferred_element_type=jnp.float32)
            * score_scale
        )
        key_part = (
            jnp.einsum("hqk,qhd->khd", score_grad, query_block, preferred_element_type=jnp.float32)
            * score_scale
        )
        value_part = jnp.einsum(
            "hqk,qhd->khd",
            chances.astype(jnp.bfloat16),
            grad_block,
            preferred_element_type=jnp.float32,
        )
        key_grad = lax.dynamic_update_slice_in_dim(
            key_grad,
            lax.dynamic_slice_in_dim(key_grad, first_row, key_span, 0) + key_part,
            first_row,
            0,
        )
        value_grad = lax.dynamic_update_slice_in_dim(
            value_grad,
            lax.dynamic_slice_in_dim(value_grad, first_row, key_span, 0) + value_part,
            first_row,
            0,
        )
        return ((key_grad, value_grad), query_grad)

    empty_grad = jnp.zeros((token_count + WINDOW, head_count, head_width), jnp.float32)
    (key_grad, value_grad), query_grad = lax.scan(
        one_block,
        (empty_grad, empty_grad),
        (jnp.arange(token_count // block_rows, dtype=jnp.int32), logsum),
    )
    flat_width = head_count * head_width
    return (
        query_grad.reshape(token_count, flat_width).astype(jnp.bfloat16),
        key_grad[WINDOW:].reshape(token_count, flat_width).astype(jnp.bfloat16),
        value_grad[WINDOW:].reshape(token_count, flat_width).astype(jnp.bfloat16),
    )


def local(
    tokens,
    cotangent,
    route,
    lengths,
    key_mask,
    norm1_gain,
    norm2_gain,
    w_query,
    w_key,
    w_value,
    w_out,
    w_gate,
    w_up,
    w_down,
):
    groups = lax.axis_size("dp")
    members = lax.axis_size("mp")
    member = lax.axis_index("mp")
    local_rows = tokens.shape[0]
    group_rows = local_rows * members
    bucket = local_rows // groups
    target = route // TOK_DEV
    chosen = (target[:, None] == jnp.arange(groups, dtype=jnp.int32)[None, :]).astype(jnp.int32)
    ranking = jnp.sum((jnp.cumsum(chosen, axis=0) - chosen) * chosen, axis=1)
    send_at = target * bucket + ranking
    arrival, arrival_grad, arrival_slot = (
        lax.all_to_all(
            jnp.zeros_like(tokens).at[send_at].set(tokens),
            "dp",
            split_axis=0,
            concat_axis=0,
            tiled=True,
        ),
        lax.all_to_all(
            jnp.zeros_like(cotangent).at[send_at].set(cotangent),
            "dp",
            split_axis=0,
            concat_axis=0,
            tiled=True,
        ),
        lax.all_to_all(
            jnp.zeros_like(route).at[send_at].set(route % local_rows),
            "dp",
            split_axis=0,
            concat_axis=0,
            tiled=True,
        ),
    )
    token_rows = jnp.zeros_like(arrival).at[arrival_slot].set(arrival)
    grad_rows = jnp.zeros_like(arrival_grad).at[arrival_slot].set(arrival_grad)
    seq_ends = jnp.cumsum(lengths[0])
    positions = jnp.arange(group_rows, dtype=jnp.int32)
    segment = jnp.sum((positions[:, None] >= seq_ends[None, :]).astype(jnp.int32), axis=1)
    input_rows = token_rows.astype(jnp.float32)
    normed_one, inverse_one = norm_rows(input_rows)
    leading_all, grad_all = (
        lax.all_gather(token_rows, "mp", axis=0, tiled=True),
        lax.all_gather(grad_rows, "mp", axis=0, tiled=True),
    )
    input_all = leading_all.astype(jnp.float32)
    normed_all, _ = norm_rows(input_all)
    hidden_one = (normed_all * norm1_gain).astype(jnp.bfloat16)
    head_count = w_query.shape[1] // HEAD_DIM
    query = jnp.dot(hidden_one, w_query, preferred_element_type=jnp.float32).astype(jnp.bfloat16)
    keys = jnp.dot(hidden_one, w_key, preferred_element_type=jnp.float32).astype(jnp.bfloat16)
    values = jnp.dot(hidden_one, w_value, preferred_element_type=jnp.float32).astype(jnp.bfloat16)
    query_heads = query.reshape(group_rows, head_count, HEAD_DIM)
    key_heads = keys.reshape(group_rows, head_count, HEAD_DIM)
    value_heads = values.reshape(group_rows, head_count, HEAD_DIM)
    mixed_flat, logsum = attend_forward(query_heads, key_heads, value_heads, segment, key_mask)
    attention_all = lax.psum(jnp.dot(mixed_flat, w_out, preferred_element_type=jnp.float32), "mp")
    middle_all = input_all + attention_all
    middle_rows = lax.dynamic_slice_in_dim(middle_all, member * local_rows, local_rows, 0)
    normed_mid, _ = norm_rows(middle_all)
    hidden_two = (normed_mid * norm2_gain).astype(jnp.bfloat16)
    normed_two, inverse_two = norm_rows(middle_rows)
    gate_value = jnp.dot(hidden_two, w_gate, preferred_element_type=jnp.float32)
    upward = jnp.dot(hidden_two, w_up, preferred_element_type=jnp.float32)
    sigmoid = jax.nn.sigmoid(gate_value)
    activated = (gate_value * sigmoid * upward).astype(jnp.bfloat16)
    out_rows = middle_rows + lax.psum_scatter(
        jnp.dot(activated, w_down, preferred_element_type=jnp.float32).astype(jnp.bfloat16),
        "mp",
        scatter_dimension=0,
        tiled=True,
    ).astype(jnp.float32)
    activated_grad = jnp.einsum("td,fd->tf", grad_all, w_down, preferred_element_type=jnp.float32)
    gate_grad = (activated_grad * upward * sigmoid * (1.0 + gate_value * (1.0 - sigmoid))).astype(
        jnp.bfloat16
    )
    upward_grad = (activated_grad * gate_value * sigmoid).astype(jnp.bfloat16)
    down_sum = jnp.einsum("tf,td->fd", activated, grad_all, preferred_element_type=jnp.float32)
    gate_sum = jnp.einsum("td,tf->df", hidden_two, gate_grad, preferred_element_type=jnp.float32)
    upward_sum = jnp.einsum(
        "td,tf->df", hidden_two, upward_grad, preferred_element_type=jnp.float32
    )
    hidden_two_grad = lax.psum_scatter(
        jnp.einsum("tf,df->td", gate_grad, w_gate, preferred_element_type=jnp.float32)
        + jnp.einsum("tf,df->td", upward_grad, w_up, preferred_element_type=jnp.float32),
        "mp",
        scatter_dimension=0,
        tiled=True,
    )
    norm_part_two, gain_two_grad = norm_back(hidden_two_grad, normed_two, inverse_two, norm2_gain)
    middle_grad = grad_rows.astype(jnp.float32) + norm_part_two
    branch_all = lax.all_gather(middle_grad.astype(jnp.bfloat16), "mp", axis=0, tiled=True)
    output_sum = jnp.einsum("tc,td->cd", mixed_flat, branch_all, preferred_element_type=jnp.float32)
    mixed_grad = jnp.einsum(
        "td,cd->tc", branch_all, w_out, preferred_element_type=jnp.float32
    ).astype(jnp.bfloat16)
    query_grad, key_grad, value_grad = attend_backward(
        query_heads,
        key_heads,
        value_heads,
        segment,
        key_mask,
        logsum,
        mixed_grad.reshape(group_rows, head_count, HEAD_DIM),
    )
    query_sum = jnp.einsum("td,tc->dc", hidden_one, query_grad, preferred_element_type=jnp.float32)
    key_sum = jnp.einsum("td,tc->dc", hidden_one, key_grad, preferred_element_type=jnp.float32)
    value_sum = jnp.einsum("td,tc->dc", hidden_one, value_grad, preferred_element_type=jnp.float32)
    hidden_one_grad = lax.psum_scatter(
        (
            jnp.einsum("tc,dc->td", query_grad, w_query, preferred_element_type=jnp.float32)
            + jnp.einsum("tc,dc->td", key_grad, w_key, preferred_element_type=jnp.float32)
            + jnp.einsum("tc,dc->td", value_grad, w_value, preferred_element_type=jnp.float32)
        ).astype(jnp.bfloat16),
        "mp",
        scatter_dimension=0,
        tiled=True,
    ).astype(jnp.float32)
    norm_part_one, gain_one_grad = norm_back(hidden_one_grad, normed_one, inverse_one, norm1_gain)
    input_grad = middle_grad + norm_part_one
    gain_one_sum, gain_two_sum = lax.psum((gain_one_grad, gain_two_grad), ("dp", "mp"))
    weight_sums = (
        lax.psum(query_sum.astype(jnp.bfloat16), "dp").astype(jnp.float32),
        lax.psum(key_sum.astype(jnp.bfloat16), "dp").astype(jnp.float32),
        lax.psum(value_sum.astype(jnp.bfloat16), "dp").astype(jnp.float32),
        lax.psum(output_sum.astype(jnp.bfloat16), "dp").astype(jnp.float32),
        lax.psum(gate_sum.astype(jnp.bfloat16), "dp").astype(jnp.float32),
        lax.psum(upward_sum.astype(jnp.bfloat16), "dp").astype(jnp.float32),
        lax.psum(down_sum.astype(jnp.bfloat16), "dp").astype(jnp.float32),
    )
    back_out, back_grad = (
        lax.all_to_all(
            out_rows.astype(jnp.bfloat16)[arrival_slot],
            "dp",
            split_axis=0,
            concat_axis=0,
            tiled=True,
        ),
        lax.all_to_all(
            input_grad.astype(jnp.bfloat16)[arrival_slot],
            "dp",
            split_axis=0,
            concat_axis=0,
            tiled=True,
        ),
    )
    return (
        back_out[send_at],
        back_grad[send_at],
        gain_one_sum,
        gain_two_sum,
        weight_sums[0],
        weight_sums[1],
        weight_sums[2],
        weight_sums[3],
        weight_sums[4],
        weight_sums[5],
        weight_sums[6],
    )


def solution(mesh):
    in_specs = (
        P(("dp", "mp"), None),
        P(("dp", "mp"), None),
        P(("dp", "mp")),
        P("dp", None),
        P("dp"),
        P(),
        P(),
        P(None, "mp"),
        P(None, "mp"),
        P(None, "mp"),
        P("mp", None),
        P(None, "mp"),
        P(None, "mp"),
        P("mp", None),
    )
    out_specs = (
        P(("dp", "mp"), None),
        P(("dp", "mp"), None),
        P(),
        P(),
        P(None, "mp"),
        P(None, "mp"),
        P(None, "mp"),
        P("mp", None),
        P(None, "mp"),
        P(None, "mp"),
        P("mp", None),
    )
    return jax.shard_map(local, mesh=mesh, in_specs=in_specs, out_specs=out_specs, check_vma=False)
```

profile of v0, /device:TPU:0, one launch (start us, length us, event | category | flops | bytes accessed | tf_op | source)
XLA Modules:
  0.0 1727.3 jit_solution(16116755077285871703)
XLA Ops:
  12.9 5.2 all-to-all-start
  18.0 4.6 scatter_custom_fusion.1
  28.3 17.6 %all-to-all-done.1 = bf16[8,48,1792]{2,1,0:T(8,128)(2,1)S(1)} async-done(((bf16[8,48,1792]{2,1,0:T(8,128)(2,1)}), bf16[8,48,1792]{2,1,0:T(8,128)(2,1)S(1)}, u32[]{:S(2)}, u32[]{:S(2)}) %all-to-all-start.1) | async-done | bytes 1376288 | tf_op jit(solution)/shard_map/all_to_all | solution.py:183
  50.2 101.4 %all-gather.4.cloned.1.call-done = bf16[1536,1792]{1,0:T(8,128)(2,1)} async-done(((bf16[384,1792]{1,0:T(8,128)(2,1)}), bf16[1536,1792]{1,0:T(8,128)(2,1)}) %all-gather.4.cloned.1.call-update) | async-done | bytes 5505040 | tf_op jit(solution)/shard_map/all_gather | solution.py:213
  169.8 26.9 %while.30 = (s32[]{:T(128)}, bf16[3,512,4,112]{1,3,2,0:T(8,128)(2,1)}, f32[3,4,512]{2,1,0:T(4,128)S(1)}, s32[3]{0:T(128)S(1)}, bf16[1600,4,112]{0,2,1:T(8,128)(2...) while((s32[]{:T(128)}, ...), condition=%wide.region_12.13_spmd, body=%wide.region_9.12_spmd.sunk | while | flops 545521280 | bytes 17490852 | solution.py:81
  204.2 7.9 fusion.83
  212.2 4.6 scatter_custom_fusion.3
  216.8 23.1 %all_to_all.60 = bf16[8,48,1792]{2,1,0:T(8,128)(2,1)} all-to-all(bf16[8,48,1792]{2,1,0:T(8,128)(2,1)} %bitcast.130), channel_id=1, replica_groups=mesh['dp'=8,'mp'=4] {'dp'}, dimensions={0} | all-to-all | bytes 2752512 | tf_op jit(solution)/shard_map/all_to_all | solution.py:190
  240.0 4.6 scatter_custom_fusion.4
  244.6 341.4 %all-reduce.9.cloned.1.call-done = f32[1536,1792]{1,0:T(8,128)} async-done(((f32[1536,1792]{1,0:T(8,128)}), f32[1536,1792]{1,0:T(8,128)}) %all-reduce.9.cloned.1.call-update) | async-done | bytes 11010064 | tf_op jit(solution)/shard_map/psum | solution.py:227
  586.1 11.9 multiply_reduce_fusion.1
  597.9 5.1 multiply_convert_fusion.1
  603.1 11.5 fusion.84
  614.6 7.7 fusion.85
  622.3 66.7 %all-gather.6.cloned.1.call-done = bf16[1536,1792]{1,0:T(8,128)(2,1)} async-done(((bf16[384,1792]{1,0:T(8,128)(2,1)}), bf16[1536,1792]{1,0:T(8,128)(2,1)}) %all-gather.6.cloned.1.call-update) | async-done | bytes 5505040 | tf_op jit(solution)/shard_map/all_gather | solution.py:214
  689.0 16.0 multiply_convert_fusion.2
  705.1 8.5 fusion.86
  713.6 11.2 convolution_add_fusion
  726.9 182.8 %reduce-scatter.6.cloned.1.call-done = f32[384,1792]{1,0:T(8,128)} async-done(((f32[1536,1792]{1,0:T(8,128)}), f32[384,1792]{1,0:T(8,128)}) %reduce-scatter.6.cloned.1.call-update) | async-done | bytes 2752528 | tf_op jit(solution)/shard_map/reduce_scatter | solution.py:253
  918.2 103.5 %all-gather.8.cloned.1.call-done = bf16[1536,1792]{1,0:T(8,128)(2,1)} async-done(((bf16[384,1792]{1,0:T(8,128)(2,1)}), bf16[1536,1792]{1,0:T(8,128)(2,1)}) %all-gather.8.cloned.1.call-update) | async-done | bytes 5505040 | tf_op jit(solution)/shard_map/all_gather | solution.py:262
  1021.8 7.1 convolution_convert_fusion.8
  1032.5 127.1 %while.31 = (s32[]{:T(128)}, f32[1600,4,112]{0,2,1:T(8,128)}, f32[1600,4,112]{0,2,1:T(8,128)}, bf16[3,512,4,112]{1,3,2,0:T(8,128)(2,1)}, s32[3]{0:T(128)S(1)}, /...) while((s32[]{:T(128)}, f32[1600,4,112]{0,2,1:T(8,128)}, ...), condition=%wide.region_24.25_spmd, body=%wide.region_22.24_spmd.sunk | while | flops 1342557824 | bytes 73204776 | solution.py:143
  1033.8 4.5 fusion.164
  1039.1 4.7 multiply_reduce_fusion.6
  1049.1 9.8 dynamic_update_slice.44
  1063.3 9.8 dynamic_update_slice.45
  1077.4 4.5 fusion.164
  1082.8 4.7 multiply_reduce_fusion.6
  1092.8 9.7 dynamic_update_slice.44
  1106.8 9.7 dynamic_update_slice.45
  1126.2 4.6 multiply_reduce_fusion.6
  1136.0 8.1 dynamic_update_slice.44
  1148.5 8.1 dynamic_update_slice.45
  1165.0 4.9 fusion.87
  1172.4 5.7 fusion.88
  1180.5 7.5 add_convert_fusion
  1188.0 10.1 convolution_convert_fusion
  1198.2 10.7 convolution_convert_fusion.1
  1209.0 10.3 convolution_convert_fusion.3
  1219.3 7.4 convolution_convert_fusion.2
  1243.9 40.6 %reduce-scatter.8.cloned.1.call-done = bf16[384,1792]{1,0:T(8,128)(2,1)} async-done(((bf16[1536,1792]{1,0:T(8,128)(2,1)}), bf16[384,1792]{1,0:T(8,128)(2,1)}) %reduce-scatter.8.cloned.1.call-update) | async-done | bytes 1376272 | tf_op jit(solution)/shard_map/reduce_scatter | solution.py:279
  1286.8 99.1 %reduce-scatter.4.cloned.1.call-done = bf16[384,1792]{1,0:T(8,128)(2,1)} async-done(((bf16[1536,1792]{1,0:T(8,128)(2,1)}), bf16[384,1792]{1,0:T(8,128)(2,1)}) %reduce-scatter.4.cloned.1.call-update) | async-done | bytes 1376272 | tf_op jit(solution)/shard_map/reduce_scatter | solution.py:237
  1385.9 5.2 fusion.63
  1400.7 30.8 %all-to-all-done.2 = bf16[8,48,1792]{2,1,0:T(8,128)(2,1)S(1)} async-done(((bf16[8,48,1792]{2,1,0:T(8,128)(2,1)}), bf16[8,48,1792]{2,1,0:T(8,128)(2,1)S(1)}, u32[]{:S(2)}, u32[]{:S(2)}) %all-to-all-start.2) | async-done | bytes 1376288 | tf_op jit(solution)/shard_map/all_to_all | solution.py:302
  1431.5 4.6 all-to-all-start.4
  1436.1 213.3 %all-reduce.11.cloned.1.call-done = (bf16[1792,448]{0,1:T(8,128)(2,1)}, bf16[1792,448]{0,1:T(8,128)(2,1)}, bf16[1792,448]{0,1:T(8,128)(2,1)}, bf16[448,1792]{1,0...) async-done(((bf16[1792,448]{0,1:T(8,128)(2,1)}, bf16[1792,448]{0,1:T(8,128)(2,1)}, bf16[1792,448]{0,1:T(8,128)(2,1)}, ...) | async-done | bytes 17432592 | tf_op jit(solution)/shard_map/psum | solution.py:293
  1671.4 39.4 %all-reduce.4 = (f32[1792]{0:T(1024)}, f32[1792]{0:T(1024)}) all-reduce(f32[1792]{0:T(1024)S(1)} %get-tuple-element.307, f32[1792]{0:T(1024)S(1)} %copy-done.27), channel_id=1, replica_groups=mesh['dp'=8,'mp'=4] {'dp','mp'}, use_global_device_ids=true, to_apply=%region_28.29 | all-reduce | flops 3584 | bytes 28672 | tf_op jit(solution)/shard_map/psum | solution.py:291
  1713.8 6.2 gather_fusion.3
  (281 shorter events, 191.4 us)
Async XLA Ops:
  7.2 197.1 %copy-start = (bf16[448,1792]{1,0:T(8,128)(2,1)S(1)}, bf16[448,1792]{1,0:T(8,128)(2,1)}, u32[]{:S(2)}) copy-start(bf16[448,1792]{1,0:T(8,128)(2,1)} %param.28) | copy-start | bytes 4816900
  9.3 203.0 %copy-start.30 = (s32[384]{0:T(512)}, s32[384]{0:T(512)S(1)}, u32[]{:S(2)}) copy-start(s32[384]{0:T(512)S(1)} %compare_select_fusion.1) | copy-start | bytes 4612
  12.9 9.8 all-to-all-start
  22.6 27.1 %copy-start.41 = (s32[1,3]{1,0:T(1,128)S(1)}, s32[1,3]{1,0:T(1,128)}, u32[]{:S(2)}) copy-start(s32[1,3]{1,0:T(1,128)} %param.21) | copy-start | bytes 40
  22.6 27.3 %copy-start.34 = (s32[1536]{0:T(1024)S(1)}, s32[1536]{0:T(1024)}, u32[]{:S(2)}) copy-start(s32[1536]{0:T(1024)} %param.22) | copy-start | bytes 18436
  22.6 23.2 %all-to-all-start.1 = ((bf16[8,48,1792]{2,1,0:T(8,128)(2,1)}), bf16[8,48,1792]{2,1,0:T(8,128)(2,1)S(1)}, u32[]{:S(2)}, u32[]{:S(2)}) async-start(bf16[8,48,1792]{2,1,0:T(8,128)(2,1)} %bitcast.14), calls=%async_computation.1 | async-start | bytes 2752512 | tf_op jit(solution)/shard_map/all_to_all | solution.py:183
  26.9 124.7 %all-gather.4.cloned.1.call-start = ((), (), s32[]{:S(2)}) async-start(), calls=%async_computation.8 | async-start | bytes 6881280 | tf_op jit(solution)/shard_map/all_gather | solution.py:213
  28.3 211.7 %copy-start.32 = (s32[384]{0:T(512)}, s32[384]{0:T(512)S(1)}, u32[]{:S(2)}) copy-start(s32[384]{0:T(512)S(1)} %fusion.79) | copy-start | bytes 4612
  49.7 536.4 %all-reduce.9.cloned.1.call-start = ((), (), s32[]{:S(2)}) async-start(), calls=%async_computation.9 | async-start | bytes 22020096 | tf_op jit(solution)/shard_map/psum | solution.py:227
  50.2 105.3 %copy-start.23 = (f32[1792]{0:T(1024)S(1)}, f32[1792]{0:T(1024)}, u32[]{:S(2)}) copy-start(f32[1792]{0:T(1024)} %param.23) | copy-start | bytes 21508
  157.2 7.3 copy-start.8
  212.2 476.8 %all-gather.6.cloned.1.call-start = ((), (), s32[]{:S(2)}) async-start(), calls=%async_computation.11 | async-start | bytes 6881280 | tf_op jit(solution)/shard_map/all_gather | solution.py:214
  244.6 353.4 %copy-start.21 = (f32[1792]{0:T(1024)S(1)}, f32[1792]{0:T(1024)}, u32[]{:S(2)}) copy-start(f32[1792]{0:T(1024)} %param.24) | copy-start | bytes 21508
  244.6 665.2 %reduce-scatter.6.cloned.1.call-start = ((), (), s32[]{:S(2)}) async-start(), calls=%async_computation.12 | async-start | bytes 13762560 | tf_op jit(solution)/shard_map/reduce_scatter | solution.py:253
  603.1 11.6 copy-start.7
  603.1 11.6 copy-start.36
  689.0 16.0 copy-start.35
  705.0 8.6 copy-start.44
  705.0 8.6 copy-start.42
  705.0 8.6 copy-start.37
  724.8 297.0 %all-gather.8.cloned.1.call-start = ((), (), s32[]{:S(2)}) async-start(), calls=%async_computation.13 | async-start | bytes 6881280 | tf_op jit(solution)/shard_map/all_gather | solution.py:262
  726.9 186.9 %copy-start.25 = (f32[384]{0:T(512)}, f32[384]{0:T(512)S(1)}, u32[]{:S(2)}) copy-start(f32[384]{0:T(512)S(1)} %add_rsqrt_fusion.3) | copy-start | bytes 4612
  909.7 4.7 copy-start.6
  918.2 366.3 %reduce-scatter.8.cloned.1.call-start = ((), (), s32[]{:S(2)}) async-start(), calls=%async_computation.14 | async-start | bytes 6881280 | tf_op jit(solution)/shard_map/reduce_scatter | solution.py:279
  1039.1 4.7 slice-start
  1039.1 4.7 slice-start.1
  1082.8 4.7 slice-start
  1082.8 4.7 slice-start.1
  1172.4 5.7 copy-start.19
  1188.0 197.9 %reduce-scatter.4.cloned.1.call-start = ((), (), s32[]{:S(2)}) async-start(), calls=%async_computation.10 | async-start | bytes 6881280 | tf_op jit(solution)/shard_map/reduce_scatter | solution.py:237
  1198.1 451.2 %all-reduce.11.cloned.1.call-start = ((), (), s32[]{:S(2)}) async-start(), calls=%async_computation.15 | async-start | bytes 34865152 | tf_op jit(solution)/shard_map/psum | solution.py:293
  1198.2 10.8 copy-start.45
  1198.2 21.1 %slice-start.2 = ((s8[5505024]{0:T(1024)(128)(4,1)}), s8[4194304]{0:T(1024)(128)(4,1)S(1)}, s32[]{:S(2)}) async-start(s8[5505024]{0:T(1024)(128)(4,1)} %bitcast.124), calls=%async_computation.18 | async-start | bytes 8388608
  1208.9 10.3 slice-start.3
  1208.9 10.3 copy-start.43
  1208.9 17.8 %slice-start.4 = ((s8[5505024]{0:T(1024)(128)(4,1)}), s8[4194304]{0:T(1024)(128)(4,1)S(1)}, s32[]{:S(2)}) async-start(s8[5505024]{0:T(1024)(128)(4,1)} %bitcast.128), calls=%async_computation.20 | async-start | bytes 8388608
  1219.3 7.4 slice-start.5
  1219.3 7.4 copy-start.20
  1226.7 11.6 slice-start.6
  1230.5 7.8 slice-start.7
  1242.2 42.3 %copy-start.24 = (f32[1792]{0:T(1024)S(1)}, f32[1792]{0:T(1024)}, u32[]{:S(2)}) copy-start(f32[1792]{0:T(1024)} %param.23) | copy-start | bytes 21508
  1242.8 143.1 %copy-start.22 = (f32[1792]{0:T(1024)S(1)}, f32[1792]{0:T(1024)}, u32[]{:S(2)}) copy-start(f32[1792]{0:T(1024)} %param.24) | copy-start | bytes 21508
  1242.8 143.1 %copy-start.26 = (f32[384]{0:T(512)S(1)}, f32[384]{0:T(512)}, u32[]{:S(2)}) copy-start(f32[384]{0:T(512)} %copy-done.25) | copy-start | bytes 4612
  1242.8 143.1 %copy-start.29 = (f32[384]{0:T(512)S(1)}, f32[384]{0:T(512)}, u32[]{:S(2)}) copy-start(f32[384]{0:T(512)} %copy-done.28) | copy-start | bytes 4612
  1394.1 37.5 %all-to-all-start.2 = ((bf16[8,48,1792]{2,1,0:T(8,128)(2,1)}), bf16[8,48,1792]{2,1,0:T(8,128)(2,1)S(1)}, u32[]{:S(2)}, u32[]{:S(2)}) async-start(bf16[8,48,1792]{2,1,0:T(8,128)(2,1)} %bitcast.127), calls=%async_computation.3 | async-start | bytes 2752512 | tf_op jit(solution)/shard_map/all_to_all | solution.py:302
  1400.7 35.4 %copy-start.31 = (s32[384]{0:T(512)S(1)}, s32[384]{0:T(512)}, u32[]{:S(2)}) copy-start(s32[384]{0:T(512)} %copy-done.30) | copy-start | bytes 4612
  1431.5 282.3 %all-to-all-start.4 = ((bf16[8,48,1792]{2,1,0:T(8,128)(2,1)}), bf16[8,48,1792]{2,1,0:T(8,128)(2,1)}, u32[]{:S(2)}, u32[]{:S(2)}) async-start(bf16[8,48,1792]{2,1,0:T(8,128)(2,1)} %bitcast.126), calls=%async_computation.7 | async-start | bytes 2752512 | tf_op jit(solution)/shard_map/all_to_all | solution.py:309
  1713.8 6.2 copy-start.1
  (24 other events, 66.9 us)
Sparse Core Ops, SparseCore 0:
  49.8 101.7 all-gather.3
  212.3 373.7 all-reduce.8
  587.6 101.3 all-gather.5
  724.9 184.7 reduce-scatter.5
  918.3 103.4 all-gather.7
  1188.1 96.3 reduce-scatter.7
  1287.3 98.5 reduce-scatter.3
  1391.7 257.6 all-reduce.10
where the time goes:
time: 1740 us; the launch traced here: 1730 us
  waiting for transfers between devices  1200 us (69%)
  matrix products  226 us (13%)
  local copies, waits for them, and re-layouts  130 us (7%)
  other arithmetic  74.3 us (4%)
  blocking collectives  62.6 us (4%)
  starting transfers between devices  18 us (1%)
    psum x1, waiting for transfers between devices, local(): lax.psum(jnp.dot(mixed_flat, w_out, preferred_element_type=jnp.float32),...  341 us
    psum x1, waiting for transfers between devices, local(): lax.psum(query_sum.astype(jnp.bfloat16), 'dp').astype(jnp.float32)  213 us
    reduce_scatter x1, waiting for transfers between devices, local(): lax.psum_scatter(jnp.einsum('tf,df->td', gate_grad, w_gate, preferred_ele...  183 us
    all_gather x1, waiting for transfers between devices, local(): lax.all_gather(middle_grad.astype(jnp.bfloat16), 'mp', axis=0, tiled=True)  104 us
    all_gather x1, waiting for transfers between devices, local(): lax.all_gather(token_rows, 'mp', axis=0, tiled=True)  101 us
    reduce_scatter x1, waiting for transfers between devices, local(): lax.psum_scatter(jnp.dot(activated, w_down, preferred_element_type=jnp.fl...  99.1 us
    all_gather x1, waiting for transfers between devices, local(): lax.all_gather(grad_rows, 'mp', axis=0, tiled=True)  66.7 us
    reduce_scatter x1, waiting for transfers between devices, local(): lax.psum_scatter((jnp.einsum('tc,dc->td', query_grad, w_query, preferred_...  40.6 us
  transfers between devices with their start and end apart: 12, of which 10 were waited for; matrix products, arithmetic and copies ran while one was open for 8% of the time, Pallas kernels for 0%

commit v1 on v0

--- a/solution.py
+++ b/solution.py
@@ -288,7 +288,7 @@
     ).astype(jnp.float32)
     norm_part_one, gain_one_grad = norm_back(hidden_one_grad, normed_one, inverse_one, norm1_gain)
     input_grad = middle_grad + norm_part_one
-    gain_one_sum, gain_two_sum = lax.psum((gain_one_grad, gain_two_grad), ("dp", "mp"))
+    gain_one_sum, gain_two_sum = lax.psum(lax.psum((gain_one_grad, gain_two_grad), "mp"), "dp")
     weight_sums = (
         lax.psum(query_sum.astype(jnp.bfloat16), "dp").astype(jnp.float32),
         lax.psum(key_sum.astype(jnp.bfloat16), "dp").astype(jnp.float32),

time: 1740 us -> 1740 us (level)
    psum x1 -> x2, blocking collectives: 39.4 us -> 41.6 us  [the longest x1 22.9 us: local(): lax.psum(lax.psum((gain_one_grad, gain_two_grad), 'mp'), 'dp')]
where the time goes in v1:
time: 1740 us; the launch traced here: 1730 us
  waiting for transfers between devices  1200 us (69%)
  matrix products  226 us (13%)
  local copies, waits for them, and re-layouts  129 us (7%)
  other arithmetic  74.3 us (4%)
  blocking collectives  64.8 us (4%)
  starting transfers between devices  18 us (1%)
    psum x1, waiting for transfers between devices, local(): lax.psum(jnp.dot(mixed_flat, w_out, preferred_element_type=jnp.float32),...  341 us
    psum x1, waiting for transfers between devices, local(): lax.psum(query_sum.astype(jnp.bfloat16), 'dp').astype(jnp.float32)  213 us
    reduce_scatter x1, waiting for transfers between devices, local(): lax.psum_scatter(jnp.einsum('tf,df->td', gate_grad, w_gate, preferred_ele...  183 us
    all_gather x1, waiting for transfers between devices, local(): lax.all_gather(middle_grad.astype(jnp.bfloat16), 'mp', axis=0, tiled=True)  104 us
    all_gather x1, waiting for transfers between devices, local(): lax.all_gather(token_rows, 'mp', axis=0, tiled=True)  101 us
    reduce_scatter x1, waiting for transfers between devices, local(): lax.psum_scatter(jnp.dot(activated, w_down, preferred_element_type=jnp.fl...  99.1 us
    all_gather x1, waiting for transfers between devices, local(): lax.all_gather(grad_rows, 'mp', axis=0, tiled=True)  66.7 us
    reduce_scatter x1, waiting for transfers between devices, local(): lax.psum_scatter((jnp.einsum('tc,dc->td', query_grad, w_query, preferred_...  40.6 us
  transfers between devices with their start and end apart: 12, of which 10 were waited for; matrix products, arithmetic and copies ran while one was open for 8% of the time, Pallas kernels for 0%

profile of v1, /device:TPU:0, one launch (start us, length us, event | category | flops | bytes accessed | tf_op | source)
XLA Modules:
  0.0 1728.4 jit_solution(17893738782248803331)
XLA Ops:
  12.9 5.2 all-to-all-start
  18.0 4.6 scatter_custom_fusion.1
  28.3 17.6 %all-to-all-done.1 = bf16[8,48,1792]{2,1,0:T(8,128)(2,1)S(1)} async-done(((bf16[8,48,1792]{2,1,0:T(8,128)(2,1)}), bf16[8,48,1792]{2,1,0:T(8,128)(2,1)S(1)}, u32[]{:S(2)}, u32[]{:S(2)}) %all-to-all-start.1) | async-done | bytes 1376288 | tf_op jit(solution)/shard_map/all_to_all | solution.py:183
  50.2 101.4 %all-gather.4.cloned.1.call-done = bf16[1536,1792]{1,0:T(8,128)(2,1)} async-done(((bf16[384,1792]{1,0:T(8,128)(2,1)}), bf16[1536,1792]{1,0:T(8,128)(2,1)}) %all-gather.4.cloned.1.call-update) | async-done | bytes 5505040 | tf_op jit(solution)/shard_map/all_gather | solution.py:213
  169.8 26.9 %while.30 = (s32[]{:T(128)}, bf16[3,512,4,112]{1,3,2,0:T(8,128)(2,1)}, f32[3,4,512]{2,1,0:T(4,128)S(1)}, s32[3]{0:T(128)S(1)}, bf16[1600,4,112]{0,2,1:T(8,128)(2...) while((s32[]{:T(128)}, ...), condition=%wide.region_12.13_spmd, body=%wide.region_9.12_spmd.sunk | while | flops 545521280 | bytes 17490852 | solution.py:81
  204.3 7.9 fusion.83
  212.3 4.6 scatter_custom_fusion.3
  216.9 23.1 %all_to_all.60 = bf16[8,48,1792]{2,1,0:T(8,128)(2,1)} all-to-all(bf16[8,48,1792]{2,1,0:T(8,128)(2,1)} %bitcast.130), channel_id=1, replica_groups=mesh['dp'=8,'mp'=4] {'dp'}, dimensions={0} | all-to-all | bytes 2752512 | tf_op jit(solution)/shard_map/all_to_all | solution.py:190
  240.0 4.6 scatter_custom_fusion.4
  244.7 341.4 %all-reduce.10.cloned.1.call-done = f32[1536,1792]{1,0:T(8,128)} async-done(((f32[1536,1792]{1,0:T(8,128)}), f32[1536,1792]{1,0:T(8,128)}) %all-reduce.10.cloned.1.call-update) | async-done | bytes 11010064 | tf_op jit(solution)/shard_map/psum | solution.py:227
  586.1 11.9 multiply_reduce_fusion.1
  598.0 5.1 multiply_convert_fusion.1
  603.1 11.6 fusion.84
  614.7 7.7 fusion.85
  622.4 66.7 %all-gather.6.cloned.1.call-done = bf16[1536,1792]{1,0:T(8,128)(2,1)} async-done(((bf16[384,1792]{1,0:T(8,128)(2,1)}), bf16[1536,1792]{1,0:T(8,128)(2,1)}) %all-gather.6.cloned.1.call-update) | async-done | bytes 5505040 | tf_op jit(solution)/shard_map/all_gather | solution.py:214
  689.1 16.0 multiply_convert_fusion.2
  705.1 8.5 fusion.86
  713.6 11.2 convolution_add_fusion
  726.9 182.8 %reduce-scatter.6.cloned.1.call-done = f32[384,1792]{1,0:T(8,128)} async-done(((f32[1536,1792]{1,0:T(8,128)}), f32[384,1792]{1,0:T(8,128)}) %reduce-scatter.6.cloned.1.call-update) | async-done | bytes 2752528 | tf_op jit(solution)/shard_map/reduce_scatter | solution.py:253
  918.3 103.5 %all-gather.8.cloned.1.call-done = bf16[1536,1792]{1,0:T(8,128)(2,1)} async-done(((bf16[384,1792]{1,0:T(8,128)(2,1)}), bf16[1536,1792]{1,0:T(8,128)(2,1)}) %all-gather.8.cloned.1.call-update) | async-done | bytes 5505040 | tf_op jit(solution)/shard_map/all_gather | solution.py:262
  1021.8 7.1 convolution_convert_fusion.8
  1032.5 127.1 %while.31 = (s32[]{:T(128)}, f32[1600,4,112]{0,2,1:T(8,128)}, f32[1600,4,112]{0,2,1:T(8,128)}, bf16[3,512,4,112]{1,3,2,0:T(8,128)(2,1)}, s32[3]{0:T(128)S(1)}, /...) while((s32[]{:T(128)}, f32[1600,4,112]{0,2,1:T(8,128)}, ...), condition=%wide.region_24.25_spmd, body=%wide.region_22.24_spmd.sunk | while | flops 1342557824 | bytes 73204776 | solution.py:143
  1033.8 4.5 fusion.164
  1039.2 4.7 multiply_reduce_fusion.6
  1049.1 9.8 dynamic_update_slice.44
  1063.3 9.8 dynamic_update_slice.45
  1082.8 4.7 multiply_reduce_fusion.6
  1092.8 9.7 dynamic_update_slice.44
  1106.8 9.7 dynamic_update_slice.45
  1126.2 4.6 multiply_reduce_fusion.6
  1136.0 8.1 dynamic_update_slice.44
  1148.4 8.1 dynamic_update_slice.45
  1163.8 5.0 fusion.87
  1171.2 5.7 fusion.88
  1179.3 7.4 add_convert_fusion
  1186.9 10.1 convolution_convert_fusion
  1197.0 10.7 convolution_convert_fusion.1
  1207.8 10.3 convolution_convert_fusion.3
  1218.2 7.4 convolution_convert_fusion.2
  1242.7 40.6 %reduce-scatter.8.cloned.1.call-done = bf16[384,1792]{1,0:T(8,128)(2,1)} async-done(((bf16[1536,1792]{1,0:T(8,128)(2,1)}), bf16[384,1792]{1,0:T(8,128)(2,1)}) %reduce-scatter.8.cloned.1.call-update) | async-done | bytes 1376272 | tf_op jit(solution)/shard_map/reduce_scatter | solution.py:279
  1285.6 99.1 %reduce-scatter.4.cloned.1.call-done = bf16[384,1792]{1,0:T(8,128)(2,1)} async-done(((bf16[1536,1792]{1,0:T(8,128)(2,1)}), bf16[384,1792]{1,0:T(8,128)(2,1)}) %reduce-scatter.4.cloned.1.call-update) | async-done | bytes 1376272 | tf_op jit(solution)/shard_map/reduce_scatter | solution.py:237
  1384.8 5.2 fusion.63
  1399.6 30.8 %all-to-all-done.2 = bf16[8,48,1792]{2,1,0:T(8,128)(2,1)S(1)} async-done(((bf16[8,48,1792]{2,1,0:T(8,128)(2,1)}), bf16[8,48,1792]{2,1,0:T(8,128)(2,1)S(1)}, u32[]{:S(2)}, u32[]{:S(2)}) %all-to-all-start.2) | async-done | bytes 1376288 | tf_op jit(solution)/shard_map/all_to_all | solution.py:302
  1430.4 4.6 all-to-all-start.4
  1435.0 213.3 %all-reduce.12.cloned.1.call-done = (bf16[1792,448]{0,1:T(8,128)(2,1)}, bf16[1792,448]{0,1:T(8,128)(2,1)}, bf16[1792,448]{0,1:T(8,128)(2,1)}, bf16[448,1792]{1,0...) async-done(((bf16[1792,448]{0,1:T(8,128)(2,1)}, bf16[1792,448]{0,1:T(8,128)(2,1)}, bf16[1792,448]{0,1:T(8,128)(2,1)}, ...) | async-done | bytes 17432592 | tf_op jit(solution)/shard_map/psum | solution.py:293
  1670.2 18.7 %all-reduce.5 = (f32[1792]{0:T(1024)S(1)}, f32[1792]{0:T(1024)S(1)}) all-reduce(f32[1792]{0:T(1024)S(1)} %get-tuple-element.307, f32[1792]{0:T(1024)S(1)} %copy-done.28), channel_id=1, replica_groups=mesh['dp'=8,'mp'=4] {'mp'}, use_global_device_ids=true, to_apply=%region_28.29 | all-reduce | flops 3584 | bytes 28672 | tf_op jit(solution)/shard_map/psum | solution.py:291
  1689.0 22.9 %all-reduce.4 = (f32[1792]{0:T(1024)}, f32[1792]{0:T(1024)}) all-reduce(f32[1792]{0:T(1024)S(1)} %get-tuple-element.357, f32[1792]{0:T(1024)S(1)} %get-tuple-element.358), channel_id=1, replica_groups=mesh['dp'=8,'mp'=4] {'dp'}, use_global_device_ids=true, to_apply=%region_29.30 | all-reduce | flops 3584 | bytes 28672 | tf_op jit(solution)/shard_map/psum | solution.py:291
  1714.8 6.2 gather_fusion.3
  (284 shorter events, 194.6 us)
Async XLA Ops:
  7.2 197.1 %copy-start = (bf16[448,1792]{1,0:T(8,128)(2,1)S(1)}, bf16[448,1792]{1,0:T(8,128)(2,1)}, u32[]{:S(2)}) copy-start(bf16[448,1792]{1,0:T(8,128)(2,1)} %param.28) | copy-start | bytes 4816900
  9.3 203.0 %copy-start.31 = (s32[384]{0:T(512)}, s32[384]{0:T(512)S(1)}, u32[]{:S(2)}) copy-start(s32[384]{0:T(512)S(1)} %compare_select_fusion.1) | copy-start | bytes 4612
  12.9 9.8 all-to-all-start
  22.6 27.1 %copy-start.42 = (s32[1,3]{1,0:T(1,128)S(1)}, s32[1,3]{1,0:T(1,128)}, u32[]{:S(2)}) copy-start(s32[1,3]{1,0:T(1,128)} %param.21) | copy-start | bytes 40
  22.6 27.3 %copy-start.35 = (s32[1536]{0:T(1024)S(1)}, s32[1536]{0:T(1024)}, u32[]{:S(2)}) copy-start(s32[1536]{0:T(1024)} %param.22) | copy-start | bytes 18436
  22.6 23.2 %all-to-all-start.1 = ((bf16[8,48,1792]{2,1,0:T(8,128)(2,1)}), bf16[8,48,1792]{2,1,0:T(8,128)(2,1)S(1)}, u32[]{:S(2)}, u32[]{:S(2)}) async-start(bf16[8,48,1792]{2,1,0:T(8,128)(2,1)} %bitcast.14), calls=%async_computation.1 | async-start | bytes 2752512 | tf_op jit(solution)/shard_map/all_to_all | solution.py:183
  26.9 124.7 %all-gather.4.cloned.1.call-start = ((), (), s32[]{:S(2)}) async-start(), calls=%async_computation.8 | async-start | bytes 6881280 | tf_op jit(solution)/shard_map/all_gather | solution.py:213
  28.3 211.7 %copy-start.33 = (s32[384]{0:T(512)}, s32[384]{0:T(512)S(1)}, u32[]{:S(2)}) copy-start(s32[384]{0:T(512)S(1)} %fusion.79) | copy-start | bytes 4612
  49.7 536.4 %all-reduce.10.cloned.1.call-start = ((), (), s32[]{:S(2)}) async-start(), calls=%async_computation.9 | async-start | bytes 22020096 | tf_op jit(solution)/shard_map/psum | solution.py:227
  50.2 105.3 %copy-start.24 = (f32[1792]{0:T(1024)S(1)}, f32[1792]{0:T(1024)}, u32[]{:S(2)}) copy-start(f32[1792]{0:T(1024)} %param.23) | copy-start | bytes 21508
  157.2 7.4 copy-start.8
  212.2 476.8 %all-gather.6.cloned.1.call-start = ((), (), s32[]{:S(2)}) async-start(), calls=%async_computation.11 | async-start | bytes 6881280 | tf_op jit(solution)/shard_map/all_gather | solution.py:214
  244.6 353.4 %copy-start.22 = (f32[1792]{0:T(1024)S(1)}, f32[1792]{0:T(1024)}, u32[]{:S(2)}) copy-start(f32[1792]{0:T(1024)} %param.24) | copy-start | bytes 21508
  244.6 665.2 %reduce-scatter.6.cloned.1.call-start = ((), (), s32[]{:S(2)}) async-start(), calls=%async_computation.12 | async-start | bytes 13762560 | tf_op jit(solution)/shard_map/reduce_scatter | solution.py:253
  603.1 11.6 copy-start.7
  603.1 11.6 copy-start.37
  689.1 16.0 copy-start.36
  705.1 8.6 copy-start.45
  705.1 8.6 copy-start.43
  705.1 8.6 copy-start.38
  724.8 297.0 %all-gather.8.cloned.1.call-start = ((), (), s32[]{:S(2)}) async-start(), calls=%async_computation.13 | async-start | bytes 6881280 | tf_op jit(solution)/shard_map/all_gather | solution.py:262
  726.9 186.9 %copy-start.26 = (f32[384]{0:T(512)}, f32[384]{0:T(512)S(1)}, u32[]{:S(2)}) copy-start(f32[384]{0:T(512)S(1)} %add_rsqrt_fusion.3) | copy-start | bytes 4612
  918.2 365.1 %reduce-scatter.8.cloned.1.call-start = ((), (), s32[]{:S(2)}) async-start(), calls=%async_computation.14 | async-start | bytes 6881280 | tf_op jit(solution)/shard_map/reduce_scatter | solution.py:279
  1039.1 4.7 slice-start
  1039.1 4.7 slice-start.1
  1082.8 4.7 slice-start
  1082.8 4.7 slice-start.1
  1163.8 5.0 copy-start.18
  1171.2 5.7 copy-start.20
  1186.8 197.9 %reduce-scatter.4.cloned.1.call-start = ((), (), s32[]{:S(2)}) async-start(), calls=%async_computation.10 | async-start | bytes 6881280 | tf_op jit(solution)/shard_map/reduce_scatter | solution.py:237
  1197.0 451.2 %all-reduce.12.cloned.1.call-start = ((), (), s32[]{:S(2)}) async-start(), calls=%async_computation.15 | async-start | bytes 34865152 | tf_op jit(solution)/shard_map/psum | solution.py:293
  1197.0 10.8 copy-start.46
  1197.0 21.1 %slice-start.2 = ((s8[5505024]{0:T(1024)(128)(4,1)}), s8[4194304]{0:T(1024)(128)(4,1)S(1)}, s32[]{:S(2)}) async-start(s8[5505024]{0:T(1024)(128)(4,1)} %bitcast.124), calls=%async_computation.18 | async-start | bytes 8388608
  1207.8 10.3 slice-start.3
  1207.8 10.3 copy-start.44
  1207.8 17.8 %slice-start.4 = ((s8[5505024]{0:T(1024)(128)(4,1)}), s8[4194304]{0:T(1024)(128)(4,1)S(1)}, s32[]{:S(2)}) async-start(s8[5505024]{0:T(1024)(128)(4,1)} %bitcast.128), calls=%async_computation.20 | async-start | bytes 8388608
  1218.1 7.5 slice-start.5
  1218.1 7.4 copy-start.21
  1225.6 11.6 slice-start.6
  1229.3 7.8 slice-start.7
  1241.0 42.3 %copy-start.25 = (f32[1792]{0:T(1024)S(1)}, f32[1792]{0:T(1024)}, u32[]{:S(2)}) copy-start(f32[1792]{0:T(1024)} %param.23) | copy-start | bytes 21508
  1241.7 143.1 %copy-start.23 = (f32[1792]{0:T(1024)S(1)}, f32[1792]{0:T(1024)}, u32[]{:S(2)}) copy-start(f32[1792]{0:T(1024)} %param.24) | copy-start | bytes 21508
  1241.7 143.1 %copy-start.27 = (f32[384]{0:T(512)S(1)}, f32[384]{0:T(512)}, u32[]{:S(2)}) copy-start(f32[384]{0:T(512)} %copy-done.26) | copy-start | bytes 4612
  1241.7 143.1 %copy-start.30 = (f32[384]{0:T(512)S(1)}, f32[384]{0:T(512)}, u32[]{:S(2)}) copy-start(f32[384]{0:T(512)} %copy-done.29) | copy-start | bytes 4612
  1392.9 37.5 %all-to-all-start.2 = ((bf16[8,48,1792]{2,1,0:T(8,128)(2,1)}), bf16[8,48,1792]{2,1,0:T(8,128)(2,1)S(1)}, u32[]{:S(2)}, u32[]{:S(2)}) async-start(bf16[8,48,1792]{2,1,0:T(8,128)(2,1)} %bitcast.127), calls=%async_computation.3 | async-start | bytes 2752512 | tf_op jit(solution)/shard_map/all_to_all | solution.py:302
  1399.6 35.4 %copy-start.32 = (s32[384]{0:T(512)S(1)}, s32[384]{0:T(512)}, u32[]{:S(2)}) copy-start(s32[384]{0:T(512)} %copy-done.31) | copy-start | bytes 4612
  1430.4 284.5 %all-to-all-start.4 = ((bf16[8,48,1792]{2,1,0:T(8,128)(2,1)}), bf16[8,48,1792]{2,1,0:T(8,128)(2,1)}, u32[]{:S(2)}, u32[]{:S(2)}) async-start(bf16[8,48,1792]{2,1,0:T(8,128)(2,1)} %bitcast.126), calls=%async_computation.7 | async-start | bytes 2752512 | tf_op jit(solution)/shard_map/all_to_all | solution.py:309
  1714.8 6.2 copy-start.1
  (25 other events, 71.6 us)
Sparse Core Ops, SparseCore 0:
  49.8 101.7 all-gather.3
  212.3 373.7 all-reduce.9
  587.7 101.3 all-gather.5
  724.9 184.7 reduce-scatter.5
  918.3 103.4 all-gather.7
  1186.9 96.3 reduce-scatter.7
  1286.2 98.5 reduce-scatter.3
  1390.5 257.6 all-reduce.11
